TPU v7x, 32 devices: a whole 2x2x4 slice. The times are simulated.
32 devices in a mesh: energy: 8 (over y, x, core), cuts: 4 (over z).
Axes of the slice: x: 2, y: 2, z: 4, core: 2. Of those that a mesh axis runs over, the one named last changes fastest.
Arguments:
- green_diag: bfloat16 [4, 32, 2, 256, 256], P('cuts', 'energy'), may hold values from -0.375 to 0.375
- green_upper: bfloat16 [4, 32, 2, 256, 256], P('cuts', 'energy'), may hold values from -0.375 to 0.375
- sigma_lesser: bfloat16 [4, 32, 2, 256, 256], P('cuts', 'energy'), may hold values from -6 to 6
- screening: bfloat16 [4, 32, 2, 256, 256], P('cuts', 'energy'), may hold values from -0.375 to 0.375
Outputs:
- polar_screened: bfloat16 [4, 32, 2, 256, 256], P('cuts', 'energy')
All inputs are finite; a program needn't handle non-finite values.
Results may differ from a plain program's by a relative error of at most 0.013.
Values may be sent and summed in bfloat16 or wider, within the bound.
A program may use at most 64 MiB of HBM per device.

v0:
```python
import math
import jax
import jax.numpy as jnp
from jax import lax
from jax.sharding import PartitionSpec as P


def shifted(value, axis, steps):
    count = lax.axis_size(axis)
    leading, last = (max(0, -steps), min(count, count - steps))
    return lax.ppermute(value, axis, [(source, source + steps) for source in range(leading, last)])


def times_block(left, right):
    real = jnp.einsum(
        "eij,ejk->eik", left[:, 0], right[:, 0], preferred_element_type=jnp.float32
    ) - jnp.einsum("eij,ejk->eik", left[:, 1], right[:, 1], preferred_element_type=jnp.float32)
    imag = jnp.einsum(
        "eij,ejk->eik", left[:, 0], right[:, 1], preferred_element_type=jnp.float32
    ) + jnp.einsum("eij,ejk->eik", left[:, 1], right[:, 0], preferred_element_type=jnp.float32)
    return jnp.stack([real, imag], axis=1)


def times_adjoint(left, right):
    real = jnp.einsum(
        "eij,ekj->eik", left[:, 0], right[:, 0], preferred_element_type=jnp.float32
    ) + jnp.einsum("eij,ekj->eik", left[:, 1], right[:, 1], preferred_element_type=jnp.float32)
    imag = jnp.einsum(
        "eij,ekj->eik", left[:, 1], right[:, 0], preferred_element_type=jnp.float32
    ) - jnp.einsum("eij,ekj->eik", left[:, 0], right[:, 1], preferred_element_type=jnp.float32)
    return jnp.stack([real, imag], axis=1)


def angle_table(rows_count, cols_count, period):
    row_index = lax.broadcasted_iota(jnp.int32, (rows_count, cols_count), 0)
    col_index = lax.broadcasted_iota(jnp.int32, (rows_count, cols_count), 1)
    phase = (row_index * col_index % period).astype(jnp.float32)
    return phase * (2.0 * math.pi / period)


def split_table_dot(table, data):
    upper = table.astype(jnp.bfloat16)
    lower = (table - upper.astype(jnp.float32)).astype(jnp.bfloat16)
    return jnp.dot(upper, data, preferred_element_type=jnp.float32) + jnp.dot(
        lower, data, preferred_element_type=jnp.float32
    )


def correlate(spread):
    energies = spread.shape[0]
    period = 2 * energies
    forward = angle_table(period, energies, period)
    inverse = angle_table(energies, period, period)
    cos_inv = jnp.cos(inverse)
    sin_inv = jnp.sin(inverse)
    high = lax.Precision.HIGHEST
    real_part = spread[:, 0].reshape(energies, -1)
    imag_part = spread[:, 1].reshape(energies, -1)
    width = real_part.shape[1]
    joined = jnp.concatenate([real_part, imag_part], axis=1)
    cos_both = split_table_dot(jnp.cos(forward), joined)
    sin_both = split_table_dot(jnp.sin(forward), joined)
    spec_real = cos_both[:, :width] + sin_both[:, width:]
    spec_imag = cos_both[:, width:] - sin_both[:, :width]
    power = spec_real * spec_real + spec_imag * spec_imag
    lag_real = jnp.dot(cos_inv, power, precision=high) / period
    lag_imag = jnp.dot(sin_inv, power, precision=high) / period
    polar = jnp.stack([lag_real, lag_imag], axis=1) / energies
    return polar.reshape(spread.shape).astype(jnp.bfloat16)


def shards(green_diag, green_upper, sigma_lesser, screening):
    sigma_next = shifted(sigma_lesser, "cuts", -1)
    own_term = times_block(green_diag[0], sigma_lesser[0]).astype(jnp.bfloat16)
    pair_term = times_block(green_upper[0], sigma_next[0]).astype(jnp.bfloat16)
    lesser = (
        times_adjoint(own_term, green_diag[0]) + times_adjoint(pair_term, green_upper[0])
    ).astype(jnp.bfloat16)
    entries = lax.all_to_all(lesser, "energy", split_axis=2, concat_axis=0, tiled=True)
    polar_rows = correlate(entries)
    back_field = lax.all_to_all(polar_rows, "energy", split_axis=0, concat_axis=2, tiled=True)
    screened_left = times_block(screening[0], back_field).astype(jnp.bfloat16)
    result_field = times_adjoint(screened_left, screening[0]).astype(jnp.bfloat16)
    return result_field[None]


def solution(mesh):
    in_specs = (
        P("cuts", "energy", None, None, None),
        P("cuts", "energy", None, None, None),
        P("cuts", "energy", None, None, None),
        P("cuts", "energy", None, None, None),
    )
    out_specs = P("cuts", "energy", None, None, None)
    return jax.shard_map(shards, mesh=mesh, in_specs=in_specs, out_specs=out_specs, check_vma=False)
```

profile of v0, /device:TPU:0, one launch (start us, length us, event | category | flops | bytes accessed | tf_op | source)
XLA Modules:
  0.0 84.3 jit_solution(1953093069969859186)
XLA Ops:
  0.0 1.4 %copy.97 = bf16[1,4,2,256,256]{4,3,1,2,0:T(8,128)(2,1)S(1)} copy(bf16[1,4,2,256,256]{4,3,2,1,0:T(8,128)(2,1)} %param.6) | data formatting | bytes 2097152 | tf_op args[2]
  1.4 1.3 %collective-permute-start = (bf16[1,4,2,256,256]{4,3,1,2,0:T(8,128)(2,1)S(1)}, bf16[1,4,2,256,256]{4,3,1,2,0:T(8,128)(2,1)S(1)}, u32[]{:S(2)}, u32[]{:S(2)}) collective-permute-start(bf16[1,4,2,256,256]{4,3,1,2,0:T(8,128)(2,1)S(1)} %copy.97), channel_id=1, source_target_pairs={{1,0},{2,1},{3,2},{5,4},{6,5},{7,6},{9,8},{10,9},{11,10},{13,12},{... | collective-permute-start | bytes 3145736 | tf_op jit(solution)/shard_map/ppermute | solution.py:11
  4.0 0.6 copy-done.1
  5.0 0.3 fusion.8
  5.3 0.3 fusion.25
  5.7 0.3 fusion.7
  6.0 23.5 %collective-permute-done = bf16[1,4,2,256,256]{4,3,1,2,0:T(8,128)(2,1)S(1)} collective-permute-done((bf16[1,4,2,256,256]{4,3,1,2,0:T(8,128)(2,1)S(1)}, bf16[1,4,2,256,256]{4,3,1,2,0:T(8,128)(2,1)S(1)}, u32[]{:S(2)}, u32[]{:S(2)}) %collective-permute-start) | collective-permute-done | bytes 1048608 | tf_op jit(solution)/shard_map/ppermute | solution.py:11
  31.1 0.3 fusion.27
  31.4 0.3 fusion.6
  31.7 0.3 fusion.5
  32.1 0.4 fusion.3
  32.5 0.8 copy.65
  33.3 19.0 %all_to_all.36 = bf16[4,2,256,256]{3,0,1,2:T(4,128)(2,1)S(1)} all-to-all(bf16[4,2,256,256]{3,0,1,2:T(4,128)(2,1)S(1)} %copy.65), channel_id=1, replica_groups=mesh['energy'=8,'cuts'=4] {'energy'}, dimensions={2} | all-to-all | bytes 2097152 | tf_op jit(solution)/shard_map/all_to_all | solution.py:79
  53.4 0.8 fusion.51
  54.2 0.8 fusion.48
  55.0 0.8 convolution_add_fusion.1
  55.9 0.8 convolution_add_fusion
  56.7 0.4 fusion.1
  57.1 1.2 %convolution_multiply_fusion.1 = f32[32,8192]{1,0:T(8,128)S(1)} fusion(f32[64,8192]{1,0:T(8,128)S(1)} %fusion.1), kind=kOutput, calls=%fused_computation.3 | convolution fusion | flops 201617408 | bytes 3145728 | tf_op jit(solution)/shard_map/dot_general | solution.py:66
  58.3 1.2 %convolution_multiply_fusion = f32[32,8192]{1,0:T(8,128)S(1)} fusion(f32[64,8192]{1,0:T(8,128)S(1)} %fusion.1), kind=kOutput, calls=%fused_computation.2 | convolution fusion | flops 201617408 | bytes 3145728 | tf_op jit(solution)/shard_map/dot_general | solution.py:67
  60.1 1.3 %fusion.4 = bf16[32,2,32,256]{3,2,1,0:T(8,128)(2,1)} fusion(f32[32,1,32,256]{3,2,1,0:T(8,128)S(1)} %bitcast.167, f32[32,1,32,256]{3,2,1,0:T(8,128)S(1)} %bitcast.165), kind=kLoop, calls=%fused_computation.12 | loop fusion | flops 1572864 | bytes 3145728 | tf_op jit(solution)/shard_map/convert_element_type | solution.py:69
  61.4 3.6 %all-to-all-start.1 = ((bf16[32,2,32,256]{3,2,1,0:T(8,128)(2,1)}), bf16[32,2,32,256]{3,2,1,0:T(8,128)(2,1)S(1)}, u32[]{:S(2)}, u32[]{:S(2)}) async-start(bf16[32,2,32,256]{3,2,1,0:T(8,128)(2,1)} %fusion.4), calls=%async_computation.1 | async-start | bytes 2097152 | tf_op jit(solution)/shard_map/all_to_all | solution.py:81
  65.1 15.2 %all-to-all-done.1 = bf16[32,2,32,256]{3,2,1,0:T(8,128)(2,1)S(1)} async-done(((bf16[32,2,32,256]{3,2,1,0:T(8,128)(2,1)}), bf16[32,2,32,256]{3,2,1,0:T(8,128)(2,1)S(1)}, u32[]{:S(2)}, u32[]{:S(2)}) %all-to-all-start.1) | async-done | bytes 1048608 | tf_op jit(solution)/shard_map/all_to_all | solution.py:81
  80.4 0.3 fusion.23
  80.7 0.3 fusion.24
  81.1 0.3 fusion.13
  81.4 0.3 fusion.30
  81.8 0.3 fusion.14
  82.1 0.3 fusion.29
  82.5 0.4 fusion.18
  82.8 0.3 fusion.17
  83.3 1.0 %copy.78 = bf16[1,4,2,256,256]{4,3,2,1,0:T(8,128)(2,1)} copy(bf16[1,4,2,256,256]{4,3,1,2,0:T(8,128)(2,1)S(1)} %pad_maximum_fusion) | data formatting | bytes 2097152 | tf_op jit(solution)/shard_map/stack | solution.py:31
  (29 shorter events, 5.2 us)
Async XLA Ops:
  0.0 2.7 %copy-start = (bf16[1,4,2,256,256]{4,3,2,1,0:T(8,128)(2,1)S(1)}, bf16[1,4,2,256,256]{4,3,2,1,0:T(8,128)(2,1)}, u32[]{:S(2)}) copy-start(bf16[1,4,2,256,256]{4,3,2,1,0:T(8,128)(2,1)} %param.4) | copy-start | bytes 3145732
  1.4 28.1 %collective-permute-start = (bf16[1,4,2,256,256]{4,3,1,2,0:T(8,128)(2,1)S(1)}, bf16[1,4,2,256,256]{4,3,1,2,0:T(8,128)(2,1)S(1)}, u32[]{:S(2)}, u32[]{:S(2)}) collective-permute-start(bf16[1,4,2,256,256]{4,3,1,2,0:T(8,128)(2,1)S(1)} %copy.97), channel_id=1, source_target_pairs={{1,0},{2,1},{3,2},{5,4},{6,5},{7,6},{9,8},{10,9},{11,10},{13,12},{... | collective-permute-start | bytes 3145736 | tf_op jit(solution)/shard_map/ppermute | solution.py:11
  3.4 1.2 %copy-start.1 = (bf16[1,4,2,256,256]{4,3,2,1,0:T(8,128)(2,1)S(1)}, bf16[1,4,2,256,256]{4,3,2,1,0:T(8,128)(2,1)}, u32[]{:S(2)}) copy-start(bf16[1,4,2,256,256]{4,3,2,1,0:T(8,128)(2,1)} %param.5) | copy-start | bytes 3145732
  60.1 4.9 %copy-start.2 = (bf16[1,4,2,256,256]{4,3,2,1,0:T(8,128)(2,1)S(1)}, bf16[1,4,2,256,256]{4,3,2,1,0:T(8,128)(2,1)}, u32[]{:S(2)}) copy-start(bf16[1,4,2,256,256]{4,3,2,1,0:T(8,128)(2,1)} %param.7) | copy-start | bytes 3145732
  61.4 18.9 %all-to-all-start.1 = ((bf16[32,2,32,256]{3,2,1,0:T(8,128)(2,1)}), bf16[32,2,32,256]{3,2,1,0:T(8,128)(2,1)S(1)}, u32[]{:S(2)}, u32[]{:S(2)}) async-start(bf16[32,2,32,256]{3,2,1,0:T(8,128)(2,1)} %fusion.4), calls=%async_computation.1 | async-start | bytes 2097152 | tf_op jit(solution)/shard_map/all_to_all | solution.py:81
where the time goes:
time: 84.6 us; the launch traced here: 84.3 us
  waiting for transfers between devices  38.7 us (46%)
  blocking collectives  19 us (22%)
  matrix products  13.4 us (16%)
  local copies, waits for them, and re-layouts  5.79 us (7%)
  starting transfers between devices  4.85 us (6%)
  other arithmetic  2.23 us (3%)
    ppermute x1, waiting for transfers between devices, shifted(): lax.ppermute(value, axis, [(source, source + steps) for source in range(l...  23.5 us
    all_to_all x1, blocking collectives, shards(): lax.all_to_all(lesser, 'energy', split_axis=2, concat_axis=0, tiled=True)  19 us
    all_to_all x1, waiting for transfers between devices, shards(): lax.all_to_all(polar_rows, 'energy', split_axis=0, concat_axis=2, tiled=T...  15.2 us
    all_to_all x1, starting transfers between devices, shards(): lax.all_to_all(polar_rows, 'energy', split_axis=0, concat_axis=2, tiled=T...  3.56 us
    unnamed x15, local copies, waits for them, and re-layouts  3.45 us
  transfers between devices with their start and end apart: 2, of which 2 were waited for; matrix products, arithmetic and copies ran while one was open for 3% of the time, Pallas kernels for 0%

commit v1 on v0

--- a/solution.py
+++ b/solution.py
@@ -78,7 +78,10 @@
     ).astype(jnp.bfloat16)
     entries = lax.all_to_all(lesser, "energy", split_axis=2, concat_axis=0, tiled=True)
     polar_rows = correlate(entries)
-    back_field = lax.all_to_all(polar_rows, "energy", split_axis=0, concat_axis=2, tiled=True)
+    size = lax.axis_size("energy")
+    blocks = jnp.stack(jnp.split(polar_rows, size, axis=0), axis=0)
+    blocks = lax.all_to_all(blocks, "energy", split_axis=0, concat_axis=0)
+    back_field = jnp.concatenate(blocks, axis=2)
     screened_left = times_block(screening[0], back_field).astype(jnp.bfloat16)
     result_field = times_adjoint(screened_left, screening[0]).astype(jnp.bfloat16)
     return result_field[None]

time: 84.6 us -> 88.9 us (1.051)
  local copies, waits for them, and re-layouts: 5.79 us -> 11.1 us
  other arithmetic: 2.23 us -> 1.25 us
    unnamed x15 -> x22, local copies, waits for them, and re-layouts: 3.45 us -> 8.1 us
    convert_element_type x1, other arithmetic: 1.29 us -> 0.3 us  [correlate(): return polar.reshape(spread.shape).astype(jnp.bfloat16)]
where the time goes in v1:
time: 88.9 us; the launch traced here: 88.7 us
  waiting for transfers between devices  38.7 us (44%)
  blocking collectives  19 us (21%)
  matrix products  13.4 us (15%)
  local copies, waits for them, and re-layouts  11.1 us (12%)
  starting transfers between devices  4.85 us (5%)
  other arithmetic  1.25 us (1%)
    ppermute x1, waiting for transfers between devices, shifted(): lax.ppermute(value, axis, [(source, source + steps) for source in range(l...  23.5 us
    all_to_all x1, blocking collectives, shards(): lax.all_to_all(lesser, 'energy', split_axis=2, concat_axis=0, tiled=True)  19 us
    all_to_all x1, waiting for transfers between devices, shards(): blocks = lax.all_to_all(blocks, 'energy', split_axis=0, concat_axis=0)  15.2 us
    unnamed x22, local copies, waits for them, and re-layouts  8.1 us
    all_to_all x1, starting transfers between devices, shards(): blocks = lax.all_to_all(blocks, 'energy', split_axis=0, concat_axis=0)  3.56 us
  transfers between devices with their start and end apart: 2, of which 2 were waited for; matrix products, arithmetic and copies ran while one was open for 3% of the time, Pallas kernels for 0%

profile of v1, /device:TPU:0, one launch (start us, length us, event | category | flops | bytes accessed | tf_op | source)
XLA Modules:
  0.0 88.7 jit_solution(4998034310411438746)
XLA Ops:
  0.0 1.4 %copy.90 = bf16[1,4,2,256,256]{4,3,1,2,0:T(8,128)(2,1)S(1)} copy(bf16[1,4,2,256,256]{4,3,2,1,0:T(8,128)(2,1)} %param.6) | data formatting | bytes 2097152 | tf_op args[2]
  1.4 1.3 %collective-permute-start = (bf16[1,4,2,256,256]{4,3,1,2,0:T(8,128)(2,1)S(1)}, bf16[1,4,2,256,256]{4,3,1,2,0:T(8,128)(2,1)S(1)}, u32[]{:S(2)}, u32[]{:S(2)}) collective-permute-start(bf16[1,4,2,256,256]{4,3,1,2,0:T(8,128)(2,1)S(1)} %copy.90), channel_id=1, source_target_pairs={{1,0},{2,1},{3,2},{5,4},{6,5},{7,6},{9,8},{10,9},{11,10},{13,12},{... | collective-permute-start | bytes 3145736 | tf_op jit(solution)/shard_map/ppermute | solution.py:11
  4.0 0.6 copy-done.1
  6.0 23.5 %collective-permute-done = bf16[1,4,2,256,256]{4,3,1,2,0:T(8,128)(2,1)S(1)} collective-permute-done((bf16[1,4,2,256,256]{4,3,1,2,0:T(8,128)(2,1)S(1)}, bf16[1,4,2,256,256]{4,3,1,2,0:T(8,128)(2,1)S(1)}, u32[]{:S(2)}, u32[]{:S(2)}) %collective-permute-start) | collective-permute-done | bytes 1048608 | tf_op jit(solution)/shard_map/ppermute | solution.py:11
  32.1 0.4 fusion.3
  32.5 0.8 copy.58
  33.3 19.0 %all_to_all.23 = bf16[4,2,256,256]{3,0,1,2:T(4,128)(2,1)S(1)} all-to-all(bf16[4,2,256,256]{3,0,1,2:T(4,128)(2,1)S(1)} %copy.58), channel_id=1, replica_groups=mesh['energy'=8,'cuts'=4] {'energy'}, dimensions={2} | all-to-all | bytes 2097152 | tf_op jit(solution)/shard_map/all_to_all | solution.py:79
  53.4 0.8 fusion.59
  54.2 0.8 fusion.56
  55.0 0.8 convolution_add_fusion.1
  55.9 0.8 convolution_add_fusion
  56.7 0.4 fusion.1
  57.1 1.2 %convolution_multiply_fusion.1 = f32[32,8192]{1,0:T(8,128)S(1)} fusion(f32[64,8192]{1,0:T(8,128)S(1)} %fusion.1), kind=kOutput, calls=%fused_computation.3 | convolution fusion | flops 201617408 | bytes 3145728 | tf_op jit(solution)/shard_map/dot_general | solution.py:66
  58.3 1.2 %convolution_multiply_fusion = f32[32,8192]{1,0:T(8,128)S(1)} fusion(f32[64,8192]{1,0:T(8,128)S(1)} %fusion.1), kind=kOutput, calls=%fused_computation.2 | convolution fusion | flops 201617408 | bytes 3145728 | tf_op jit(solution)/shard_map/dot_general | solution.py:67
  60.4 0.7 fusion.38
  61.1 0.7 fusion.37
  61.8 0.7 fusion.36
  62.4 0.7 fusion.35
  63.1 0.7 fusion.34
  63.8 0.7 fusion.33
  64.4 0.7 fusion.32
  65.1 0.7 fusion.31
  65.7 3.6 %all-to-all-start.1 = ((bf16[8,4,2,32,256]{4,3,2,1,0:T(8,128)(2,1)}), bf16[8,4,2,32,256]{4,3,2,1,0:T(8,128)(2,1)S(1)}, u32[]{:S(2)}, u32[]{:S(2)}) async-start(bf16[8,4,2,32,256]{4,3,2,1,0:T(8,128)(2,1)} %fusion.31), calls=%async_computation.1 | async-start | bytes 2097152 | tf_op jit(solution)/shard_map/all_to_all | solution.py:83
  69.4 15.2 %all-to-all-done.1 = bf16[8,4,2,32,256]{4,3,2,1,0:T(8,128)(2,1)S(1)} async-done(((bf16[8,4,2,32,256]{4,3,2,1,0:T(8,128)(2,1)}), bf16[8,4,2,32,256]{4,3,2,1,0:T(8,128)(2,1)S(1)}, u32[]{:S(2)}, u32[]{:S(2)}) %all-to-all-start.1) | async-done | bytes 1048608 | tf_op jit(solution)/shard_map/all_to_all | solution.py:83
  84.7 0.3 fusion.23
  85.1 0.4 fusion.24
  85.4 0.3 fusion.13
  86.1 0.4 fusion.14
  86.5 0.3 fusion.29
  86.8 0.3 fusion.18
  87.2 0.3 fusion.17
  87.6 1.0 %copy.71 = bf16[1,4,2,256,256]{4,3,2,1,0:T(8,128)(2,1)} copy(bf16[1,4,2,256,256]{4,3,1,2,0:T(8,128)(2,1)S(1)} %pad_maximum_fusion) | data formatting | bytes 2097152 | tf_op jit(solution)/shard_map/stack | solution.py:31
  (37 shorter events, 7.8 us)
Async XLA Ops:
  0.0 2.7 %copy-start = (bf16[1,4,2,256,256]{4,3,2,1,0:T(8,128)(2,1)S(1)}, bf16[1,4,2,256,256]{4,3,2,1,0:T(8,128)(2,1)}, u32[]{:S(2)}) copy-start(bf16[1,4,2,256,256]{4,3,2,1,0:T(8,128)(2,1)} %param.4) | copy-start | bytes 3145732
  1.4 28.1 %collective-permute-start = (bf16[1,4,2,256,256]{4,3,1,2,0:T(8,128)(2,1)S(1)}, bf16[1,4,2,256,256]{4,3,1,2,0:T(8,128)(2,1)S(1)}, u32[]{:S(2)}, u32[]{:S(2)}) collective-permute-start(bf16[1,4,2,256,256]{4,3,1,2,0:T(8,128)(2,1)S(1)} %copy.90), channel_id=1, source_target_pairs={{1,0},{2,1},{3,2},{5,4},{6,5},{7,6},{9,8},{10,9},{11,10},{13,12},{... | collective-permute-start | bytes 3145736 | tf_op jit(solution)/shard_map/ppermute | solution.py:11
  3.4 1.2 %copy-start.1 = (bf16[1,4,2,256,256]{4,3,2,1,0:T(8,128)(2,1)S(1)}, bf16[1,4,2,256,256]{4,3,2,1,0:T(8,128)(2,1)}, u32[]{:S(2)}) copy-start(bf16[1,4,2,256,256]{4,3,2,1,0:T(8,128)(2,1)} %param.5) | copy-start | bytes 3145732
  60.4 8.9 %copy-start.2 = (bf16[1,4,2,256,256]{4,3,2,1,0:T(8,128)(2,1)S(1)}, bf16[1,4,2,256,256]{4,3,2,1,0:T(8,128)(2,1)}, u32[]{:S(2)}) copy-start(bf16[1,4,2,256,256]{4,3,2,1,0:T(8,128)(2,1)} %param.7) | copy-start | bytes 3145732
  65.7 18.9 %all-to-all-start.1 = ((bf16[8,4,2,32,256]{4,3,2,1,0:T(8,128)(2,1)}), bf16[8,4,2,32,256]{4,3,2,1,0:T(8,128)(2,1)S(1)}, u32[]{:S(2)}, u32[]{:S(2)}) async-start(bf16[8,4,2,32,256]{4,3,2,1,0:T(8,128)(2,1)} %fusion.31), calls=%async_computation.1 | async-start | bytes 2097152 | tf_op jit(solution)/shard_map/all_to_all | solution.py:83
